TPU v7x, 32 devices: a whole 2x2x4 slice. The times are simulated.
32 devices in a mesh: gz: 8 (over z, core), xy: 4 (over y, x).
Axes of the slice: x: 2, y: 2, z: 4, core: 2. Of those that a mesh axis runs over, the one named last changes fastest.
Arguments:
- slab_image: float32 [32, 128, 1024], P('gz', None, 'xy'), may hold values from 0 to 1
- width_taps: float32 [16, 5], replicated, may hold values from -2.5 to 2.5
- height_taps: float32 [16, 5], replicated, may hold values from -2.5 to 2.5
- depth_taps: float32 [16, 5], replicated, may hold values from -2.5 to 2.5
- fragment_ids: int32 [32, 128, 1024], P(None, 'gz', 'xy'), may hold values from 0 to 1023, as said below
- fragment_owner: int32 [32768, 1], P(('gz', 'xy')), may hold values from 0 to 3, as said below
- coarse_centroids: float32 [16, 1024], P(None, ('gz', 'xy')), may hold values from -24 to 24
- parent_map: int32 [4096], P(('gz', 'xy')), may hold values from 0 to 31
- fine_offsets: float32 [16, 4096], P(None, ('gz', 'xy')), may hold values from -2.5 to 2.5
Outputs:
- fragment_means: float32 [16, 32768], P(None, ('gz', 'xy'))
- centroids: float32 [16, 4096], P(None, ('gz', 'xy'))
Inputs may be any that keep to these rules, and one draw needn't show every extreme that they name: `fragment_ids`: ids are local to a pencil block of 32 x 16 x 256 voxels; every id 0 to 1023 occurs in every block. `fragment_owner`: of the 1024 fragments of one pencil block at most 512 name the same owner; in each row along xy some owner takes exactly 512 from every block of that row.
All inputs are finite; a program needn't handle non-finite values.
Results may differ from a plain program's by a relative error of at most 0.00038.
Values may be sent and summed in bfloat16 or wider, within the bound.
A program may use at most 128 MiB of HBM per device.

v0:
```python
import jax
import jax.numpy as jnp
from jax import lax
from jax.sharding import PartitionSpec as P

TAPS = 5
BZ = 4
ITERS = 3
HIGH = lax.Precision.HIGHEST
sharpness = 2.0
group_span = 4


def with_halo(cells, sides, width):
    for axis, dim in sides:
        count = lax.axis_size(axis)
        ends = count - 1
        head = lax.slice_in_dim(cells, 0, width, axis=dim)
        tail = lax.slice_in_dim(cells, cells.shape[dim] - width, cells.shape[dim], axis=dim)
        cells = jnp.concatenate(
            [
                lax.ppermute(tail, axis, [(i, (i + 1) % count) for i in range(ends)]),
                cells,
                lax.ppermute(head, axis, [((i + 1) % count, i) for i in range(ends)]),
            ],
            axis=dim,
        )
    return cells


def planar_filter(padded, width_taps, height_taps):
    reach = width_taps.shape[1]
    rows = padded.shape[1] - reach + 1
    cols = padded.shape[2] - reach + 1
    pieces = []
    for chan_start in range(0, width_taps.shape[0], group_span):
        width_tap = width_taps[chan_start : chan_start + group_span][:, :, None, None, None]
        height_tap = height_taps[chan_start : chan_start + group_span][:, :, None, None, None]
        across = width_tap[:, 0] * padded[None, :, :, 0:cols]
        for tap_shift in range(1, reach):
            across = (
                across + width_tap[:, tap_shift] * padded[None, :, :, tap_shift : tap_shift + cols]
            )
        planar = height_tap[:, 0] * across[:, :, 0:rows, :]
        for tap_shift in range(1, reach):
            planar = (
                planar + height_tap[:, tap_shift] * across[:, :, tap_shift : tap_shift + rows, :]
            )
        pieces.append(planar.astype(jnp.bfloat16))
    return jnp.concatenate(pieces, axis=0)


def depth_filter(planar, depth_taps):
    reach = depth_taps.shape[1]
    half = reach // 2
    depth = planar.shape[1]
    planar = lax.optimization_barrier(planar)
    pieces = []
    for chan_start in range(0, planar.shape[0], group_span):
        block = planar[chan_start : chan_start + group_span].astype(jnp.float32)
        padded = jnp.pad(block, ((0, 0), (half, half), (0, 0), (0, 0)))
        depth_tap = depth_taps[chan_start : chan_start + group_span][:, :, None, None, None]
        response = depth_tap[:, 0] * padded[:, 0:depth]
        for tap_shift in range(1, reach):
            response = response + depth_tap[:, tap_shift] * padded[:, tap_shift : tap_shift + depth]
        pieces.append(jnp.tanh(response).astype(jnp.bfloat16))
    return jnp.concatenate(pieces, axis=0)


def fragment_sums(features, fragment_ids, fragments):
    chans, depth, rows, cols = features.shape
    labels = jnp.arange(fragments, dtype=jnp.int32)
    voxels = BZ * rows * cols

    def add_block(index, carry):
        sums, counts = carry
        start = index * BZ
        block = lax.dynamic_slice_in_dim(features, start, BZ, 1).reshape(chans, voxels)
        block_ids = lax.dynamic_slice_in_dim(fragment_ids, start, BZ, 0).reshape(voxels)
        member = block_ids[:, None] == labels[None, :]
        sums = sums + jnp.dot(
            block, member.astype(jnp.bfloat16), preferred_element_type=jnp.float32
        )
        counts = counts + jnp.sum(member.astype(jnp.float32), axis=0)
        return (sums, counts)

    start_carry = (jnp.zeros((chans, fragments), jnp.float32), jnp.zeros((fragments,), jnp.float32))
    return lax.fori_loop(0, depth // BZ, add_block, start_carry)


def soft_stats(frags, weight, cents):
    cross = lax.dot_general(
        frags, cents, (((0,), (0,)), ((), ())), precision=HIGH, preferred_element_type=jnp.float32
    )
    distance = (
        jnp.sum(frags * frags, axis=0)[:, None]
        + jnp.sum(cents * cents, axis=0)[None, :]
        - 2.0 * cross
    )
    scores = -sharpness * distance
    top = jnp.max(scores, axis=1, keepdims=True)
    expo = jnp.exp(scores - top)
    resp = expo / jnp.sum(expo, axis=1, keepdims=True)
    numer = jnp.dot(
        frags * weight[None, :], resp, precision=HIGH, preferred_element_type=jnp.float32
    )
    denom = jnp.dot(weight[None, :], resp, precision=HIGH, preferred_element_type=jnp.float32)
    return (numer, denom)


def shards(
    slab_image,
    width_taps,
    height_taps,
    depth_taps,
    fragment_ids,
    fragment_owner,
    coarse_centroids,
    parent_map,
    fine_offsets,
):
    half = TAPS // 2
    rimmed = with_halo(slab_image, (("xy", 2),), TAPS // 2)
    rimmed = jnp.pad(rimmed, ((0, 0), (half, half), (0, 0)))
    planar = planar_filter(rimmed, width_taps, height_taps)
    planar = lax.all_to_all(planar, "gz", split_axis=2, concat_axis=1, tiled=True)
    features = depth_filter(planar, depth_taps)
    fragments = fragment_owner.shape[0]
    sums, counts = fragment_sums(features, fragment_ids, fragments)
    means = sums / counts[None, :]
    coarse_count = coarse_centroids.shape[1]
    select = (parent_map[None, :] == jnp.arange(coarse_count, dtype=jnp.int32)[:, None]).astype(
        jnp.float32
    )
    centroids = (
        jnp.dot(coarse_centroids, select, precision=HIGH, preferred_element_type=jnp.float32)
        + fine_offsets
    )
    fine_count = centroids.shape[1]
    pseudo = float(fragment_ids.size // fine_count)
    owner = fragment_owner[:, 0]
    lanes = lax.axis_size("xy")
    capacity = min(fragments // 2, 4 * fragments // lanes)
    pick = (owner[:, None] == jnp.arange(lanes, dtype=jnp.int32)[None, :]).astype(jnp.int32)
    rank = jnp.sum((jnp.cumsum(pick, axis=0) - 1) * pick, axis=1)
    slot = owner * capacity + rank
    packed = jnp.zeros((means.shape[0], lanes * capacity), jnp.float32).at[:, slot].set(means)
    weights = jnp.zeros((1, lanes * capacity), jnp.float32).at[0, slot].set(counts)
    arrived, arrived_weight = (
        lax.all_to_all(packed, "xy", split_axis=1, concat_axis=1, tiled=True),
        lax.all_to_all(weights, "xy", split_axis=1, concat_axis=1, tiled=True),
    )
    for step in range(ITERS):
        numer, denom = soft_stats(arrived, arrived_weight[0], centroids)
        centroids = (numer + pseudo * centroids) / (denom + pseudo)
    return (means, centroids)


def solution(mesh):
    placed = (
        P("gz", None, "xy"),
        P(),
        P(),
        P(),
        P(None, "gz", "xy"),
        P(("gz", "xy"), None),
        P(None, ("gz", "xy")),
        P(("gz", "xy")),
        P(None, ("gz", "xy")),
    )
    return jax.shard_map(
        shards,
        mesh=mesh,
        in_specs=placed,
        out_specs=(P(None, ("gz", "xy")), P(None, ("gz", "xy"))),
        check_vma=False,
    )
```

profile of v0, /device:TPU:0, one launch (start us, length us, event | category | flops | bytes accessed | tf_op | source)
XLA Modules:
  0.0 379.4 jit_solution(12561259763467322268)
XLA Ops:
  1.8 4.9 %collective-permute-start = (f32[4,128,2]{2,1,0:T(8,128)S(1)}, f32[4,128,2]{2,1,0:T(8,128)S(1)}, u32[]{:S(2)}, u32[]{:S(2)}) collective-permute-start(f32[4,128,2]{2,1,0:T(8,128)S(1)} %get-tuple-element.217), channel_id=1, source_target_pairs={{0,1},{1,2},{2,3},{4,5},{5,6},{6,7},{8,9},{9,10},{10,11},{12,13},{... | collective-permute-start | bytes 12296 | tf_op jit(solution)/shard_map/ppermute | solution.py:22
  12.2 7.6 %collective-permute-done.1 = f32[4,128,2]{2,1,0:T(8,128)S(1)} collective-permute-done((f32[4,128,2]{2,1,0:T(8,128)S(1)}, f32[4,128,2]{2,1,0:T(8,128)S(1)}, u32[]{:S(2)}, u32[]{:S(2)}) %collective-permute-start.1) | collective-permute-done | bytes 4128 | tf_op jit(solution)/shard_map/ppermute | solution.py:24
  22.9 2.9 multiply_add_fusion.3
  25.8 2.8 fusion.69
  28.6 2.8 fusion.64
  34.1 2.8 fusion.59
  39.7 4.3 %pad_maximum_fusion = bf16[16,4,128,256]{3,1,0,2:T(4,128)(2,1)} fusion(bf16[4,4,128,256]{3,1,0,2:T(4,128)(2,1)S(1)} %fusion.54, bf16[4,4,128,256]{3,1,0,2:T(4,128)(2,1)S(1)} %fusion.59, bf16[4,4,128,256]{3,1,0,2:T(4,128)(2,1)S(1)} %fusion.64, bf16[4,4,128,256]{3,1,0,2:T(4,128)(2,1)S(1)} %fusion.69), kind=kLoop, calls=%fused_computation.12 | loop fusion | flops 6291456 | bytes 8388608 | tf_op jit(solution)/shard_map/concatenate | solution.py:50
  44.1 5.0 %all-to-all-start = ((bf16[16,4,128,256]{3,1,0,2:T(4,128)(2,1)}), bf16[16,4,128,256]{3,1,0,2:T(4,128)(2,1)}, u32[]{:S(2)}, u32[]{:S(2)}) async-start(bf16[16,4,128,256]{3,1,0,2:T(4,128)(2,1)} %pad_maximum_fusion), calls=%async_computation | async-start | bytes 8388608 | tf_op jit(solution)/shard_map/all_to_all | solution.py:126
  52.5 90.7 %all-to-all-done = bf16[16,4,128,256]{3,1,0,2:T(4,128)(2,1)} async-done(((bf16[16,4,128,256]{3,1,0,2:T(4,128)(2,1)}), bf16[16,4,128,256]{3,1,0,2:T(4,128)(2,1)}, u32[]{:S(2)}, u32[]{:S(2)}) %all-to-all-start) | async-done | bytes 4194336 | tf_op jit(solution)/shard_map/all_to_all | solution.py:126
  143.2 4.6 %copy.108 = bf16[16,4,128,256]{3,2,1,0:T(8,128)(2,1)S(1)} copy(bf16[16,4,128,256]{3,1,0,2:T(4,128)(2,1)} %all-to-all-done) | data formatting | bytes 8388608 | tf_op jit(solution)/shard_map/all_to_all | solution.py:126
  155.0 193.2 %while.16 = (s32[]{:T(128)}, f32[16,1024]{1,0:T(8,128)S(1)}, f32[1024]{0:T(1024)S(1)}, bf16[16,32,16,256]{3,2,1,0:T(8,128)(2,1)}, s32[32,16,256]{2,1,0:T(8,128)}...) while((s32[]{:T(128)}, f32[16,1024]{1,0:T(8,128)S(1)}, f32[1024]{0:T(1024)S(1)}, ...), condition=%wide.region_2.3_spmd.clone, body=%wide.region_0.2_spmd.clone.sunk | while | flops 604013568 | bytes 3162270 | solution.py:88
  157.3 14.0 %fusion.132 = f32[16,1024]{1,0:T(8,128)S(1)} fusion(bf16[16,16384]{1,0:T(8,128)(2,1)S(1)} %bitcast.93, s32[16384]{0:T(1024)S(1)} %bitcast.96, f32[16,1024]{1,0:T(8,128)S(1)} %get-tuple-element.294, pred[]{:T(512)S(6)} %compare.27), kind=kOutput, calls=%fused_computation.8.clone.1 | convolution fusion | flops 553680896 | bytes 720897 | tf_op jit(solution)/shard_map/while/body/eval_jaxpr/dot_general | solution.py:81
  171.3 7.8 %fusion.133 = f32[1024]{0:T(1024)S(1)} fusion(s32[16384]{0:T(1024)S(1)} %bitcast.97), kind=kLoop, calls=%fused_computation.6.clone.1 | loop fusion | flops 50330624 | bytes 69632 | tf_op jit(solution)/shard_map/while/body/eval_jaxpr/reduce_sum | solution.py:84
  181.5 14.0 %fusion.132 = f32[16,1024]{1,0:T(8,128)S(1)} fusion(bf16[16,16384]{1,0:T(8,128)(2,1)S(1)} %bitcast.93, s32[16384]{0:T(1024)S(1)} %bitcast.96, f32[16,1024]{1,0:T(8,128)S(1)} %get-tuple-element.294, pred[]{:T(512)S(6)} %compare.27), kind=kOutput, calls=%fused_computation.8.clone.1 | convolution fusion | flops 553680896 | bytes 720897 | tf_op jit(solution)/shard_map/while/body/eval_jaxpr/dot_general | solution.py:81
  195.5 7.8 %fusion.133 = f32[1024]{0:T(1024)S(1)} fusion(s32[16384]{0:T(1024)S(1)} %bitcast.97), kind=kLoop, calls=%fused_computation.6.clone.1 | loop fusion | flops 50330624 | bytes 69632 | tf_op jit(solution)/shard_map/while/body/eval_jaxpr/reduce_sum | solution.py:84
  205.6 14.0 %fusion.132 = f32[16,1024]{1,0:T(8,128)S(1)} fusion(bf16[16,16384]{1,0:T(8,128)(2,1)S(1)} %bitcast.93, s32[16384]{0:T(1024)S(1)} %bitcast.96, f32[16,1024]{1,0:T(8,128)S(1)} %get-tuple-element.294, pred[]{:T(512)S(6)} %compare.27), kind=kOutput, calls=%fused_computation.8.clone.1 | convolution fusion | flops 553680896 | bytes 720897 | tf_op jit(solution)/shard_map/while/body/eval_jaxpr/dot_general | solution.py:81
  219.6 7.8 %fusion.133 = f32[1024]{0:T(1024)S(1)} fusion(s32[16384]{0:T(1024)S(1)} %bitcast.97), kind=kLoop, calls=%fused_computation.6.clone.1 | loop fusion | flops 50330624 | bytes 69632 | tf_op jit(solution)/shard_map/while/body/eval_jaxpr/reduce_sum | solution.py:84
  229.8 14.0 %fusion.132 = f32[16,1024]{1,0:T(8,128)S(1)} fusion(bf16[16,16384]{1,0:T(8,128)(2,1)S(1)} %bitcast.93, s32[16384]{0:T(1024)S(1)} %bitcast.96, f32[16,1024]{1,0:T(8,128)S(1)} %get-tuple-element.294, pred[]{:T(512)S(6)} %compare.27), kind=kOutput, calls=%fused_computation.8.clone.1 | convolution fusion | flops 553680896 | bytes 720897 | tf_op jit(solution)/shard_map/while/body/eval_jaxpr/dot_general | solution.py:81
  243.8 7.8 %fusion.133 = f32[1024]{0:T(1024)S(1)} fusion(s32[16384]{0:T(1024)S(1)} %bitcast.97), kind=kLoop, calls=%fused_computation.6.clone.1 | loop fusion | flops 50330624 | bytes 69632 | tf_op jit(solution)/shard_map/while/body/eval_jaxpr/reduce_sum | solution.py:84
  253.9 14.0 %fusion.132 = f32[16,1024]{1,0:T(8,128)S(1)} fusion(bf16[16,16384]{1,0:T(8,128)(2,1)S(1)} %bitcast.93, s32[16384]{0:T(1024)S(1)} %bitcast.96, f32[16,1024]{1,0:T(8,128)S(1)} %get-tuple-element.294, pred[]{:T(512)S(6)} %compare.27), kind=kOutput, calls=%fused_computation.8.clone.1 | convolution fusion | flops 553680896 | bytes 720897 | tf_op jit(solution)/shard_map/while/body/eval_jaxpr/dot_general | solution.py:81
  267.9 7.8 %fusion.133 = f32[1024]{0:T(1024)S(1)} fusion(s32[16384]{0:T(1024)S(1)} %bitcast.97), kind=kLoop, calls=%fused_computation.6.clone.1 | loop fusion | flops 50330624 | bytes 69632 | tf_op jit(solution)/shard_map/while/body/eval_jaxpr/reduce_sum | solution.py:84
  278.1 14.0 %fusion.132 = f32[16,1024]{1,0:T(8,128)S(1)} fusion(bf16[16,16384]{1,0:T(8,128)(2,1)S(1)} %bitcast.93, s32[16384]{0:T(1024)S(1)} %bitcast.96, f32[16,1024]{1,0:T(8,128)S(1)} %get-tuple-element.294, pred[]{:T(512)S(6)} %compare.27), kind=kOutput, calls=%fused_computation.8.clone.1 | convolution fusion | flops 553680896 | bytes 720897 | tf_op jit(solution)/shard_map/while/body/eval_jaxpr/dot_general | solution.py:81
  292.1 7.8 %fusion.133 = f32[1024]{0:T(1024)S(1)} fusion(s32[16384]{0:T(1024)S(1)} %bitcast.97), kind=kLoop, calls=%fused_computation.6.clone.1 | loop fusion | flops 50330624 | bytes 69632 | tf_op jit(solution)/shard_map/while/body/eval_jaxpr/reduce_sum | solution.py:84
  302.2 14.0 %fusion.132 = f32[16,1024]{1,0:T(8,128)S(1)} fusion(bf16[16,16384]{1,0:T(8,128)(2,1)S(1)} %bitcast.93, s32[16384]{0:T(1024)S(1)} %bitcast.96, f32[16,1024]{1,0:T(8,128)S(1)} %get-tuple-element.294, pred[]{:T(512)S(6)} %compare.27), kind=kOutput, calls=%fused_computation.8.clone.1 | convolution fusion | flops 553680896 | bytes 720897 | tf_op jit(solution)/shard_map/while/body/eval_jaxpr/dot_general | solution.py:81
  316.2 7.8 %fusion.133 = f32[1024]{0:T(1024)S(1)} fusion(s32[16384]{0:T(1024)S(1)} %bitcast.97), kind=kLoop, calls=%fused_computation.6.clone.1 | loop fusion | flops 50330624 | bytes 69632 | tf_op jit(solution)/shard_map/while/body/eval_jaxpr/reduce_sum | solution.py:84
  326.4 14.0 %fusion.132 = f32[16,1024]{1,0:T(8,128)S(1)} fusion(bf16[16,16384]{1,0:T(8,128)(2,1)S(1)} %bitcast.93, s32[16384]{0:T(1024)S(1)} %bitcast.96, f32[16,1024]{1,0:T(8,128)S(1)} %get-tuple-element.294, pred[]{:T(512)S(6)} %compare.27), kind=kOutput, calls=%fused_computation.8.clone.1 | convolution fusion | flops 553680896 | bytes 720897 | tf_op jit(solution)/shard_map/while/body/eval_jaxpr/dot_general | solution.py:81
  340.4 7.8 %fusion.133 = f32[1024]{0:T(1024)S(1)} fusion(s32[16384]{0:T(1024)S(1)} %bitcast.97), kind=kLoop, calls=%fused_computation.6.clone.1 | loop fusion | flops 50330624 | bytes 69632 | tf_op jit(solution)/shard_map/while/body/eval_jaxpr/reduce_sum | solution.py:84
  348.4 3.3 scatter_custom_fusion
  352.7 3.6 all-to-all-start.1
  357.0 4.9 %scatter_custom_fusion.1 = f32[2048]{0:T(1024)} fusion(s32[1024]{0:T(1024)S(1)} %broadcast_select_fusion, f32[1024]{0:T(1024)S(1)} %get-tuple-element.113, f32[]{:T(128)} %constant.57.clone.1), kind=kCustom, calls=%fused_computation.182 | custom fusion | bytes 8196
  361.8 3.9 %all-to-all-start.2 = ((f32[1,4,512]{2,0,1:T(1,128)}), f32[1,4,512]{2,0,1:T(1,128)S(1)}, u32[]{:S(2)}, u32[]{:S(2)}) async-start(f32[1,4,512]{2,0,1:T(1,128)} %bitcast.22), calls=%async_computation.2 | async-start | bytes 16384 | tf_op jit(solution)/shard_map/all_to_all | solution.py:151
  367.1 3.3 all-to-all-done.2
  (131 shorter events, 56.1 us)
Async XLA Ops:
  0.6 51.7 %copy-start = (f32[16,32]{1,0:T(8,128)S(1)}, f32[16,32]{1,0:T(8,128)}, u32[]{:S(2)}) copy-start(f32[16,32]{1,0:T(8,128)} %param.17) | copy-start | bytes 6148
  1.8 10.4 %collective-permute-start = (f32[4,128,2]{2,1,0:T(8,128)S(1)}, f32[4,128,2]{2,1,0:T(8,128)S(1)}, u32[]{:S(2)}, u32[]{:S(2)}) collective-permute-start(f32[4,128,2]{2,1,0:T(8,128)S(1)} %get-tuple-element.217), channel_id=1, source_target_pairs={{0,1},{1,2},{2,3},{4,5},{5,6},{6,7},{8,9},{9,10},{10,11},{12,13},{... | collective-permute-start | bytes 12296 | tf_op jit(solution)/shard_map/ppermute | solution.py:22
  6.7 13.1 %collective-permute-start.1 = (f32[4,128,2]{2,1,0:T(8,128)S(1)}, f32[4,128,2]{2,1,0:T(8,128)S(1)}, u32[]{:S(2)}, u32[]{:S(2)}) collective-permute-start(f32[4,128,2]{2,1,0:T(8,128)S(1)} %get-tuple-element.218), channel_id=1, source_target_pairs={{1,0},{2,1},{3,2},{5,4},{6,5},{7,6},{9,8},{10,9},{11,10},{13,12},{... | collective-permute-start | bytes 12296 | tf_op jit(solution)/shard_map/ppermute | solution.py:24
  44.1 5.1 %copy-start.1 = (f32[16,5]{0,1:T(8,128)S(1)}, f32[16,5]{0,1:T(8,128)}, u32[]{:S(2)}) copy-start(f32[16,5]{0,1:T(8,128)} %param.14) | copy-start | bytes 964
  44.1 5.5 %copy-start.2 = (s32[1024,1]{0,1:T(1,128)S(1)}, s32[1024,1]{0,1:T(1,128)}, u32[]{:S(2)}) copy-start(s32[1024,1]{0,1:T(1,128)} %param.16) | copy-start | bytes 12292
  44.1 8.1 %copy-start.5 = (s32[2]{0:T(128)S(1)}, s32[2]{0:T(128)}, u32[]{:S(2)}) copy-start(s32[2]{0:T(128)} %constant.78) | copy-start | bytes 28
  44.1 8.2 %copy-start.6 = (s32[2]{0:T(128)S(1)}, s32[2]{0:T(128)}, u32[]{:S(2)}) copy-start(s32[2]{0:T(128)} %constant.81) | copy-start | bytes 28
  44.1 8.3 %copy-start.3 = (f32[16,128]{1,0:T(8,128)S(1)}, f32[16,128]{1,0:T(8,128)}, u32[]{:S(2)}) copy-start(f32[16,128]{1,0:T(8,128)} %param.19) | copy-start | bytes 24580
  44.1 8.3 %copy-start.4 = (s32[128]{0:T(128)S(1)}, s32[128]{0:T(128)}, u32[]{:S(2)}) copy-start(s32[128]{0:T(128)} %param.18) | copy-start | bytes 1540
  44.1 99.1 %all-to-all-start = ((bf16[16,4,128,256]{3,1,0,2:T(4,128)(2,1)}), bf16[16,4,128,256]{3,1,0,2:T(4,128)(2,1)}, u32[]{:S(2)}, u32[]{:S(2)}) async-start(bf16[16,4,128,256]{3,1,0,2:T(4,128)(2,1)} %pad_maximum_fusion), calls=%async_computation | async-start | bytes 8388608 | tf_op jit(solution)/shard_map/all_to_all | solution.py:126
  352.7 9.1 %all-to-all-start.1 = ((f32[16,4,512]{2,0,1:T(8,128)}), f32[16,4,512]{2,0,1:T(8,128)S(1)}, u32[]{:S(2)}, u32[]{:S(2)}) async-start(f32[16,4,512]{2,0,1:T(8,128)} %copy.114), calls=%async_computation.1 | async-start | bytes 262144 | tf_op jit(solution)/shard_map/all_to_all | solution.py:150
  361.8 8.6 %all-to-all-start.2 = ((f32[1,4,512]{2,0,1:T(1,128)}), f32[1,4,512]{2,0,1:T(1,128)S(1)}, u32[]{:S(2)}, u32[]{:S(2)}) async-start(f32[1,4,512]{2,0,1:T(1,128)} %bitcast.22), calls=%async_computation.2 | async-start | bytes 16384 | tf_op jit(solution)/shard_map/all_to_all | solution.py:151
where the time goes:
time: 381 us; the launch traced here: 379 us
  matrix products  122 us (32%)
  waiting for transfers between devices  102 us (27%)
  other arithmetic  94.4 us (25%)
  local copies, waits for them, and re-layouts  41.2 us (11%)
  starting transfers between devices  18.7 us (5%)
    dot_general x8, matrix products, add_block(): jnp.dot(block, member.astype(jnp.bfloat16), preferred_element_type=jnp.fl...  112 us
    all_to_all x1, waiting for transfers between devices, shards(): lax.all_to_all(planar, 'gz', split_axis=2, concat_axis=1, tiled=True)  90.7 us
    reduce_sum x8, other arithmetic, add_block(): counts = counts + jnp.sum(member.astype(jnp.float32), axis=0)  62.5 us
    convert_element_type x4, other arithmetic, planar_filter(): pieces.append(planar.astype(jnp.bfloat16))  11.2 us
    dynamic_slice x8, local copies, waits for them, and re-layouts, add_block(): lax.dynamic_slice_in_dim(features, start, BZ, 1).reshape(chans, voxels)  8.71 us
  transfers between devices with their start and end apart: 5, of which 4 were waited for; matrix products, arithmetic and copies ran while one was open for 4% of the time, Pallas kernels for 0%

commit v1 on v0

--- a/solution.py
+++ b/solution.py
@@ -9,6 +9,22 @@
 HIGH = lax.Precision.HIGHEST
 sharpness = 2.0
 group_span = 4
+
+
+def pairwise_exchange(array, axis, split, join):
+    ways, here = (lax.axis_size(axis), lax.axis_index(axis))
+    width = array.shape[split] // ways
+    shape = list(array.shape)
+    shape[split] = width
+    height = shape[join]
+    shape[join] = height * ways
+    full = jnp.zeros(shape, array.dtype)
+    for mask in range(ways):
+        part = lax.dynamic_slice_in_dim(array, (here ^ mask) * width, width, axis=split)
+        if mask:
+            part = lax.ppermute(part, axis, [(d, d ^ mask) for d in range(ways)])
+        full = lax.dynamic_update_slice_in_dim(full, part, (here ^ mask) * height, axis=join)
+    return full
 
 
 def with_halo(cells, sides, width):
@@ -123,7 +139,7 @@
     rimmed = with_halo(slab_image, (("xy", 2),), TAPS // 2)
     rimmed = jnp.pad(rimmed, ((0, 0), (half, half), (0, 0)))
     planar = planar_filter(rimmed, width_taps, height_taps)
-    planar = lax.all_to_all(planar, "gz", split_axis=2, concat_axis=1, tiled=True)
+    planar = pairwise_exchange(planar, "gz", 2, 1)
     features = depth_filter(planar, depth_taps)
     fragments = fragment_owner.shape[0]
     sums, counts = fragment_sums(features, fragment_ids, fragments)

time: 381 us -> 366 us (0.961)
  the two profiles are of different devices: /device:TPU:0 before, /device:TPU:16 now
where the time goes in v1:
time: 366 us; the launch traced here: 364 us
  matrix products  123 us (34%)
  waiting for transfers between devices  88 us (24%)
  other arithmetic  87.5 us (24%)
  local copies, waits for them, and re-layouts  46 us (13%)
  starting transfers between devices  18.7 us (5%)
    dot_general x8, matrix products, add_block(): jnp.dot(block, member.astype(jnp.bfloat16), preferred_element_type=jnp.fl...  112 us
    ppermute x7, waiting for transfers between devices, pairwise_exchange(): part = lax.ppermute(part, axis, [(d, d ^ mask) for d in range(ways)])  84 us
    reduce_sum x8, other arithmetic, add_block(): counts = counts + jnp.sum(member.astype(jnp.float32), axis=0)  62.5 us
    dynamic_slice x8, local copies, waits for them, and re-layouts, add_block(): lax.dynamic_slice_in_dim(features, start, BZ, 1).reshape(chans, voxels)  8.71 us
  transfers between devices with their start and end apart: 11, of which 7 were waited for; matrix products, arithmetic and copies ran while one was open for 7% of the time, Pallas kernels for 0%

profile of v1, /device:TPU:16, one launch (start us, length us, event | category | flops | bytes accessed | tf_op | source)
XLA Modules:
  0.0 364.4 jit_solution(8025099707867173564)
XLA Ops:
  1.8 3.4 collective-permute-start
  29.0 2.3 broadcast_in_dim.40
  36.7 2.2 collective-permute-start.6
  40.6 26.2 %collective-permute-done.3 = bf16[16,4,16,256]{3,2,1,0:T(8,128)(2,1)S(1)} collective-permute-done((bf16[16,4,16,256]{3,2,1,0:T(8,128)(2,1)}, bf16[16,4,16,256]{3,2,1,0:T(8,128)(2,1)S(1)}, u32[]{:S(2)}, u32[]{:S(2)}) %collective-permute-start.3) | collective-permute-done | bytes 524320 | tf_op jit(solution)/shard_map/ppermute | solution.py:25
  68.2 9.5 %collective-permute-done.4 = bf16[16,4,16,256]{3,2,1,0:T(8,128)(2,1)S(1)} collective-permute-done((bf16[16,4,16,256]{3,2,1,0:T(8,128)(2,1)}, bf16[16,4,16,256]{3,2,1,0:T(8,128)(2,1)S(1)}, u32[]{:S(2)}, u32[]{:S(2)}) %collective-permute-start.4) | collective-permute-done | bytes 524320 | tf_op jit(solution)/shard_map/ppermute | solution.py:25
  79.4 25.8 %collective-permute-done.6 = bf16[16,4,16,256]{3,2,1,0:T(8,128)(2,1)S(1)} collective-permute-done((bf16[16,4,16,256]{3,2,1,0:T(8,128)(2,1)}, bf16[16,4,16,256]{3,2,1,0:T(8,128)(2,1)S(1)}, u32[]{:S(2)}, u32[]{:S(2)}) %collective-permute-start.6) | collective-permute-done | bytes 524320 | tf_op jit(solution)/shard_map/ppermute | solution.py:25
  106.0 13.4 %collective-permute-done.7 = bf16[16,4,16,256]{3,2,1,0:T(8,128)(2,1)S(1)} collective-permute-done((bf16[16,4,16,256]{3,2,1,0:T(8,128)(2,1)}, bf16[16,4,16,256]{3,2,1,0:T(8,128)(2,1)S(1)}, u32[]{:S(2)}, u32[]{:S(2)}) %collective-permute-start.7) | collective-permute-done | bytes 524320 | tf_op jit(solution)/shard_map/ppermute | solution.py:25
  120.3 9.1 %collective-permute-done.8 = bf16[16,4,16,256]{3,2,1,0:T(8,128)(2,1)S(1)} collective-permute-done((bf16[16,4,16,256]{3,2,1,0:T(8,128)(2,1)S(1)}, bf16[16,4,16,256]{3,2,1,0:T(8,128)(2,1)S(1)}, u32[]{:S(2)}, u32[]{:S(2)}) %collective-permute-start.8) | collective-permute-done | bytes 524320 | tf_op jit(solution)/shard_map/ppermute | solution.py:25
  130.2 3.3 slice_convert_fusion.3
  136.7 2.3 pad_maximum_fusion.1
  139.0 193.2 %while.16 = (s32[]{:T(128)}, f32[16,1024]{1,0:T(8,128)S(1)}, f32[1024]{0:T(1024)S(1)}, bf16[16,32,16,256]{3,2,1,0:T(8,128)(2,1)}, s32[32,16,256]{2,1,0:T(8,128)}...) while((s32[]{:T(128)}, f32[16,1024]{1,0:T(8,128)S(1)}, f32[1024]{0:T(1024)S(1)}, ...), condition=%wide.region_2.3_spmd.clone, body=%wide.region_0.2_spmd.clone.sunk | while | flops 604013568 | bytes 3162270 | solution.py:104
  141.3 14.0 %fusion.132 = f32[16,1024]{1,0:T(8,128)S(1)} fusion(bf16[16,16384]{1,0:T(8,128)(2,1)S(1)} %bitcast.87, s32[16384]{0:T(1024)S(1)} %bitcast.90, f32[16,1024]{1,0:T(8,128)S(1)} %get-tuple-element.302, pred[]{:T(512)S(6)} %compare.27), kind=kOutput, calls=%fused_computation.8.clone.1 | convolution fusion | flops 553680896 | bytes 720897 | tf_op jit(solution)/shard_map/while/body/eval_jaxpr/dot_general | solution.py:97
  155.3 7.8 %fusion.133 = f32[1024]{0:T(1024)S(1)} fusion(s32[16384]{0:T(1024)S(1)} %bitcast.91), kind=kLoop, calls=%fused_computation.6.clone.1 | loop fusion | flops 50330624 | bytes 69632 | tf_op jit(solution)/shard_map/while/body/eval_jaxpr/reduce_sum | solution.py:100
  165.4 14.0 %fusion.132 = f32[16,1024]{1,0:T(8,128)S(1)} fusion(bf16[16,16384]{1,0:T(8,128)(2,1)S(1)} %bitcast.87, s32[16384]{0:T(1024)S(1)} %bitcast.90, f32[16,1024]{1,0:T(8,128)S(1)} %get-tuple-element.302, pred[]{:T(512)S(6)} %compare.27), kind=kOutput, calls=%fused_computation.8.clone.1 | convolution fusion | flops 553680896 | bytes 720897 | tf_op jit(solution)/shard_map/while/body/eval_jaxpr/dot_general | solution.py:97
  179.4 7.8 %fusion.133 = f32[1024]{0:T(1024)S(1)} fusion(s32[16384]{0:T(1024)S(1)} %bitcast.91), kind=kLoop, calls=%fused_computation.6.clone.1 | loop fusion | flops 50330624 | bytes 69632 | tf_op jit(solution)/shard_map/while/body/eval_jaxpr/reduce_sum | solution.py:100
  189.6 14.0 %fusion.132 = f32[16,1024]{1,0:T(8,128)S(1)} fusion(bf16[16,16384]{1,0:T(8,128)(2,1)S(1)} %bitcast.87, s32[16384]{0:T(1024)S(1)} %bitcast.90, f32[16,1024]{1,0:T(8,128)S(1)} %get-tuple-element.302, pred[]{:T(512)S(6)} %compare.27), kind=kOutput, calls=%fused_computation.8.clone.1 | convolution fusion | flops 553680896 | bytes 720897 | tf_op jit(solution)/shard_map/while/body/eval_jaxpr/dot_general | solution.py:97
  203.6 7.8 %fusion.133 = f32[1024]{0:T(1024)S(1)} fusion(s32[16384]{0:T(1024)S(1)} %bitcast.91), kind=kLoop, calls=%fused_computation.6.clone.1 | loop fusion | flops 50330624 | bytes 69632 | tf_op jit(solution)/shard_map/while/body/eval_jaxpr/reduce_sum | solution.py:100
  213.7 14.0 %fusion.132 = f32[16,1024]{1,0:T(8,128)S(1)} fusion(bf16[16,16384]{1,0:T(8,128)(2,1)S(1)} %bitcast.87, s32[16384]{0:T(1024)S(1)} %bitcast.90, f32[16,1024]{1,0:T(8,128)S(1)} %get-tuple-element.302, pred[]{:T(512)S(6)} %compare.27), kind=kOutput, calls=%fused_computation.8.clone.1 | convolution fusion | flops 553680896 | bytes 720897 | tf_op jit(solution)/shard_map/while/body/eval_jaxpr/dot_general | solution.py:97
  227.7 7.8 %fusion.133 = f32[1024]{0:T(1024)S(1)} fusion(s32[16384]{0:T(1024)S(1)} %bitcast.91), kind=kLoop, calls=%fused_computation.6.clone.1 | loop fusion | flops 50330624 | bytes 69632 | tf_op jit(solution)/shard_map/while/body/eval_jaxpr/reduce_sum | solution.py:100
  237.9 14.0 %fusion.132 = f32[16,1024]{1,0:T(8,128)S(1)} fusion(bf16[16,16384]{1,0:T(8,128)(2,1)S(1)} %bitcast.87, s32[16384]{0:T(1024)S(1)} %bitcast.90, f32[16,1024]{1,0:T(8,128)S(1)} %get-tuple-element.302, pred[]{:T(512)S(6)} %compare.27), kind=kOutput, calls=%fused_computation.8.clone.1 | convolution fusion | flops 553680896 | bytes 720897 | tf_op jit(solution)/shard_map/while/body/eval_jaxpr/dot_general | solution.py:97
  251.9 7.8 %fusion.133 = f32[1024]{0:T(1024)S(1)} fusion(s32[16384]{0:T(1024)S(1)} %bitcast.91), kind=kLoop, calls=%fused_computation.6.clone.1 | loop fusion | flops 50330624 | bytes 69632 | tf_op jit(solution)/shard_map/while/body/eval_jaxpr/reduce_sum | solution.py:100
  262.0 14.0 %fusion.132 = f32[16,1024]{1,0:T(8,128)S(1)} fusion(bf16[16,16384]{1,0:T(8,128)(2,1)S(1)} %bitcast.87, s32[16384]{0:T(1024)S(1)} %bitcast.90, f32[16,1024]{1,0:T(8,128)S(1)} %get-tuple-element.302, pred[]{:T(512)S(6)} %compare.27), kind=kOutput, calls=%fused_computation.8.clone.1 | convolution fusion | flops 553680896 | bytes 720897 | tf_op jit(solution)/shard_map/while/body/eval_jaxpr/dot_general | solution.py:97
  276.0 7.8 %fusion.133 = f32[1024]{0:T(1024)S(1)} fusion(s32[16384]{0:T(1024)S(1)} %bitcast.91), kind=kLoop, calls=%fused_computation.6.clone.1 | loop fusion | flops 50330624 | bytes 69632 | tf_op jit(solution)/shard_map/while/body/eval_jaxpr/reduce_sum | solution.py:100
  286.2 14.0 %fusion.132 = f32[16,1024]{1,0:T(8,128)S(1)} fusion(bf16[16,16384]{1,0:T(8,128)(2,1)S(1)} %bitcast.87, s32[16384]{0:T(1024)S(1)} %bitcast.90, f32[16,1024]{1,0:T(8,128)S(1)} %get-tuple-element.302, pred[]{:T(512)S(6)} %compare.27), kind=kOutput, calls=%fused_computation.8.clone.1 | convolution fusion | flops 553680896 | bytes 720897 | tf_op jit(solution)/shard_map/while/body/eval_jaxpr/dot_general | solution.py:97
  300.2 7.8 %fusion.133 = f32[1024]{0:T(1024)S(1)} fusion(s32[16384]{0:T(1024)S(1)} %bitcast.91), kind=kLoop, calls=%fused_computation.6.clone.1 | loop fusion | flops 50330624 | bytes 69632 | tf_op jit(solution)/shard_map/while/body/eval_jaxpr/reduce_sum | solution.py:100
  310.3 14.0 %fusion.132 = f32[16,1024]{1,0:T(8,128)S(1)} fusion(bf16[16,16384]{1,0:T(8,128)(2,1)S(1)} %bitcast.87, s32[16384]{0:T(1024)S(1)} %bitcast.90, f32[16,1024]{1,0:T(8,128)S(1)} %get-tuple-element.302, pred[]{:T(512)S(6)} %compare.27), kind=kOutput, calls=%fused_computation.8.clone.1 | convolution fusion | flops 553680896 | bytes 720897 | tf_op jit(solution)/shard_map/while/body/eval_jaxpr/dot_general | solution.py:97
  324.3 7.8 %fusion.133 = f32[1024]{0:T(1024)S(1)} fusion(s32[16384]{0:T(1024)S(1)} %bitcast.91), kind=kLoop, calls=%fused_computation.6.clone.1 | loop fusion | flops 50330624 | bytes 69632 | tf_op jit(solution)/shard_map/while/body/eval_jaxpr/reduce_sum | solution.py:100
  332.4 3.3 scatter_custom_fusion
  336.7 4.2 %all-to-all-start = ((f32[16,4,512]{2,0,1:T(8,128)}), f32[16,4,512]{2,0,1:T(8,128)S(1)}, u32[]{:S(2)}, u32[]{:S(2)}) async-start(f32[16,4,512]{2,0,1:T(8,128)} %copy.79), calls=%async_computation | async-start | bytes 262144 | tf_op jit(solution)/shard_map/all_to_all | solution.py:166
  341.6 4.9 %scatter_custom_fusion.1 = f32[2048]{0:T(1024)} fusion(s32[1024]{0:T(1024)S(1)} %broadcast_select_fusion, f32[1024]{0:T(1024)S(1)} %get-tuple-element.113, f32[]{:T(128)} %constant.72.clone.1), kind=kCustom, calls=%fused_computation.183 | custom fusion | bytes 8196
  346.5 4.2 %all-to-all-start.1 = ((f32[1,4,512]{2,0,1:T(1,128)}), f32[1,4,512]{2,0,1:T(1,128)S(1)}, u32[]{:S(2)}, u32[]{:S(2)}) async-start(f32[1,4,512]{2,0,1:T(1,128)} %bitcast.19), calls=%async_computation.1 | async-start | bytes 16384 | tf_op jit(solution)/shard_map/all_to_all | solution.py:167
  352.1 3.3 all-to-all-done.1
  (133 shorter events, 70.8 us)
Async XLA Ops:
  0.6 15.9 %copy-start = (f32[16,32]{1,0:T(8,128)S(1)}, f32[16,32]{1,0:T(8,128)}, u32[]{:S(2)}) copy-start(f32[16,32]{1,0:T(8,128)} %param.17) | copy-start | bytes 6148
  1.8 15.9 %collective-permute-start = (f32[4,128,2]{2,1,0:T(8,128)S(1)}, f32[4,128,2]{2,1,0:T(8,128)S(1)}, u32[]{:S(2)}, u32[]{:S(2)}) collective-permute-start(f32[4,128,2]{2,1,0:T(8,128)S(1)} %get-tuple-element.225), channel_id=1, source_target_pairs={{0,1},{1,2},{2,3},{4,5},{5,6},{6,7},{8,9},{9,10},{10,11},{12,13},{... | collective-permute-start | bytes 12296 | tf_op jit(solution)/shard_map/ppermute | solution.py:38
  5.2 13.1 %collective-permute-start.1 = (f32[4,128,2]{2,1,0:T(8,128)S(1)}, f32[4,128,2]{2,1,0:T(8,128)S(1)}, u32[]{:S(2)}, u32[]{:S(2)}) collective-permute-start(f32[4,128,2]{2,1,0:T(8,128)S(1)} %get-tuple-element.226), channel_id=1, source_target_pairs={{1,0},{2,1},{3,2},{5,4},{6,5},{7,6},{9,8},{10,9},{11,10},{13,12},{... | collective-permute-start | bytes 12296 | tf_op jit(solution)/shard_map/ppermute | solution.py:40
  33.4 5.8 %collective-permute-start.2 = (bf16[16,4,16,256]{3,2,1,0:T(8,128)(2,1)}, bf16[16,4,16,256]{3,2,1,0:T(8,128)(2,1)S(1)}, u32[]{:S(2)}, u32[]{:S(2)}) collective-permute-start(bf16[16,4,16,256]{3,2,1,0:T(8,128)(2,1)} %get-tuple-element.214), channel_id=1, source_target_pairs={{0,4},{4,0},{8,12},{12,8},{16,20},{20,16},{24,28},{28,24},{1,5},{5... | collective-permute-start | bytes 1572872 | tf_op jit(solution)/shard_map/ppermute | solution.py:25
  33.6 33.3 %collective-permute-start.3 = (bf16[16,4,16,256]{3,2,1,0:T(8,128)(2,1)}, bf16[16,4,16,256]{3,2,1,0:T(8,128)(2,1)S(1)}, u32[]{:S(2)}, u32[]{:S(2)}) collective-permute-start(bf16[16,4,16,256]{3,2,1,0:T(8,128)(2,1)} %get-tuple-element.213), channel_id=1, source_target_pairs={{0,8},{4,12},{8,0},{12,4},{16,24},{20,28},{24,16},{28,20},{1,9},{5... | collective-permute-start | bytes 1572872 | tf_op jit(solution)/shard_map/ppermute | solution.py:25
  35.4 42.3 %collective-permute-start.4 = (bf16[16,4,16,256]{3,2,1,0:T(8,128)(2,1)}, bf16[16,4,16,256]{3,2,1,0:T(8,128)(2,1)S(1)}, u32[]{:S(2)}, u32[]{:S(2)}) collective-permute-start(bf16[16,4,16,256]{3,2,1,0:T(8,128)(2,1)} %get-tuple-element.212), channel_id=1, source_target_pairs={{0,12},{4,8},{8,4},{12,0},{16,28},{20,24},{24,20},{28,16},{1,13},{... | collective-permute-start | bytes 1572872 | tf_op jit(solution)/shard_map/ppermute | solution.py:25
  36.0 42.5 %collective-permute-start.5 = (bf16[16,4,16,256]{3,2,1,0:T(8,128)(2,1)}, bf16[16,4,16,256]{3,2,1,0:T(8,128)(2,1)S(1)}, u32[]{:S(2)}, u32[]{:S(2)}) collective-permute-start(bf16[16,4,16,256]{3,2,1,0:T(8,128)(2,1)} %get-tuple-element.211), channel_id=1, source_target_pairs={{0,16},{4,20},{8,24},{12,28},{16,0},{20,4},{24,8},{28,12},{1,17},{... | collective-permute-start | bytes 1572872 | tf_op jit(solution)/shard_map/ppermute | solution.py:25
  36.7 68.5 %collective-permute-start.6 = (bf16[16,4,16,256]{3,2,1,0:T(8,128)(2,1)}, bf16[16,4,16,256]{3,2,1,0:T(8,128)(2,1)S(1)}, u32[]{:S(2)}, u32[]{:S(2)}) collective-permute-start(bf16[16,4,16,256]{3,2,1,0:T(8,128)(2,1)} %get-tuple-element.210), channel_id=1, source_target_pairs={{0,20},{4,16},{8,28},{12,24},{16,4},{20,0},{24,12},{28,8},{1,21},{... | collective-permute-start | bytes 1572872 | tf_op jit(solution)/shard_map/ppermute | solution.py:25
  39.2 80.3 %collective-permute-start.7 = (bf16[16,4,16,256]{3,2,1,0:T(8,128)(2,1)}, bf16[16,4,16,256]{3,2,1,0:T(8,128)(2,1)S(1)}, u32[]{:S(2)}, u32[]{:S(2)}) collective-permute-start(bf16[16,4,16,256]{3,2,1,0:T(8,128)(2,1)} %get-tuple-element.209), channel_id=1, source_target_pairs={{0,24},{4,28},{8,16},{12,20},{16,8},{20,12},{24,0},{28,4},{1,25},{... | collective-permute-start | bytes 1572872 | tf_op jit(solution)/shard_map/ppermute | solution.py:25
  66.9 62.6 %collective-permute-start.8 = (bf16[16,4,16,256]{3,2,1,0:T(8,128)(2,1)S(1)}, bf16[16,4,16,256]{3,2,1,0:T(8,128)(2,1)S(1)}, u32[]{:S(2)}, u32[]{:S(2)}) collective-permute-start(bf16[16,4,16,256]{3,2,1,0:T(8,128)(2,1)S(1)} %get-tuple-element.208), channel_id=1, source_target_pairs={{0,28},{4,24},{8,20},{12,16},{16,12},{20,8},{24,4},{28,0},{1,29},{... | collective-permute-start | bytes 1572872 | tf_op jit(solution)/shard_map/ppermute | solution.py:25
  336.7 9.8 %all-to-all-start = ((f32[16,4,512]{2,0,1:T(8,128)}), f32[16,4,512]{2,0,1:T(8,128)S(1)}, u32[]{:S(2)}, u32[]{:S(2)}) async-start(f32[16,4,512]{2,0,1:T(8,128)} %copy.79), calls=%async_computation | async-start | bytes 262144 | tf_op jit(solution)/shard_map/all_to_all | solution.py:166
  346.5 8.9 %all-to-all-start.1 = ((f32[1,4,512]{2,0,1:T(1,128)}), f32[1,4,512]{2,0,1:T(1,128)S(1)}, u32[]{:S(2)}, u32[]{:S(2)}) async-start(f32[1,4,512]{2,0,1:T(1,128)} %bitcast.19), calls=%async_computation.1 | async-start | bytes 16384 | tf_op jit(solution)/shard_map/all_to_all | solution.py:167
